TPU v7x, 512 devices: a whole 4x8x8 slice. The times are simulated.
512 devices in a mesh: ctx: 32 (over y, x), mp: 16 (over z, core).
Axes of the slice: x: 4, y: 8, z: 8, core: 2. Of those that a mesh axis runs over, the one named last changes fastest.
Arguments:
- source_rows: bfloat16 [16384, 3, 8192], P('ctx', None, 'mp'), may hold values from -6 to 6
- short_filters: bfloat16 [3, 7, 8192], P(None, None, 'mp'), may hold values from -2 to 2
- medium_filters: bfloat16 [128, 512], P(None, 'mp'), may hold values from -0.5 to 0.5
- skip_gain: float32 [8192], P('mp'), may hold values from 0.1 to 1.9
- out_weight: bfloat16 [8192, 8192], P('mp', 'ctx'), may hold values from -0.0625 to 0.0625
- doc_lengths: int32 [8], replicated, may hold values from 1 to 2048, 8192 in all
- block_packing_device: int32 [32, 16], replicated, may hold values from 0 to 31, as said below
Outputs:
- mixed: bfloat16 [8192, 8192], P('ctx', 'mp')
Inputs may be any that keep to these rules, and one draw needn't show every extreme that they name: `block_packing_device`: row c names, for the 16 blocks of stretch c in order, the packing device that holds each; the entries of one row differ, and some packing device is named in every row. A packing device keeps the blocks it holds in increasing order of their stretch, in its first slots.
All inputs are finite; a program needn't handle non-finite values.
Results may differ from a plain program's by a relative error of at most 0.02.
Values may be sent and summed in bfloat16 or wider, within the bound.
No kernel may reach another device: no remote copies, remote signals or barrier semaphores. Data moves between devices by JAX's collectives and lax.ppermute only.
A program may use at most 128 MiB of HBM per device.

v0:
```python
import jax
import jax.numpy as jnp
from jax import lax
from jax.sharding import PartitionSpec as P


def passed_along(block, axis, distance):
    devices = range(lax.axis_size(axis))
    route = [(i - distance, i) for i in devices if i - distance in devices]
    return lax.ppermute(block, axis, route)


def reach_back(positions, starts):
    begin = jnp.max(jnp.where(starts[None, :] <= positions[:, None], starts[None, :], 0), axis=1)
    return positions - begin


def short_conv(extended, filt, back, count):
    span = filt.shape[0]
    taps = filt.astype(jnp.float32)
    total = jnp.zeros((count, extended.shape[1]), jnp.float32)
    for step in range(span):
        keep = (back >= step).astype(jnp.float32)[:, None]
        piece = extended[span - 1 - step : span - 1 - step + count].astype(jnp.float32)
        total = total + taps[step][None, :] * piece * keep
    return total


def on_device(
    source_rows,
    short_filters,
    medium_filters,
    skip_gain,
    out_weight,
    doc_lengths,
    block_packing_device,
):
    stretches = lax.axis_size("ctx")
    rank_me = lax.axis_index("ctx")
    nb_own = block_packing_device.shape[1]
    blk = source_rows.shape[0] // stretches
    rows = nb_own * blk
    width = source_rows.shape[2]
    se_len = short_filters.shape[1]
    mr_len = medium_filters.shape[0]
    member = jnp.any(block_packing_device == rank_me, axis=1)
    flags = member.astype(jnp.int32)
    slots = jnp.cumsum(flags) - flags
    blocks = source_rows.reshape(stretches, blk, 3, width)
    outgoing = jnp.where(
        member[:, None, None, None], jnp.take(blocks, slots, axis=0), jnp.zeros((), jnp.bfloat16)
    )
    incoming = lax.all_to_all(outgoing, "ctx", split_axis=0, concat_axis=0, tiled=True)
    wanted = lax.dynamic_index_in_dim(block_packing_device, rank_me, 0, keepdims=False)
    stretch = jnp.take(incoming, wanted, axis=0).reshape(rows, 3, width)
    ends = jnp.cumsum(doc_lengths)
    starts = ends - doc_lengths
    base = rank_me * rows
    positions = base + jnp.arange(rows, dtype=jnp.int32)
    back = reach_back(positions, starts)
    span_cols = rows + mr_len - 1
    edge = stretch[rows - (se_len - 1) :]
    earlier = passed_along(edge, "ctx", 1)
    extended = jnp.concatenate([earlier, stretch], axis=0)
    query = short_conv(extended[:, 0], short_filters[0], back, rows)
    keyed = short_conv(extended[:, 1], short_filters[1], back, rows)
    valued = short_conv(extended[:, 2], short_filters[2], back, rows)
    z_vals = (keyed * valued).astype(jnp.bfloat16)
    z_prev = passed_along(z_vals[rows - (mr_len - 1) :], "ctx", 1)
    z_ext = jnp.concatenate([z_prev, z_vals], axis=0)
    groups_dev = medium_filters.shape[1]
    per_group = width // groups_dev
    reversed_taps = jnp.transpose(medium_filters[::-1])
    line = jnp.concatenate([reversed_taps, jnp.zeros((groups_dev, rows), jnp.bfloat16)], axis=1)
    band = jnp.tile(line, (1, rows + 1))[:, : rows * span_cols].reshape(groups_dev, rows, span_cols)
    ext_pos = base - (mr_len - 1) + jnp.arange(span_cols, dtype=jnp.int32)
    begin_rows = positions - back
    keep = ext_pos[None, :] >= begin_rows[:, None]
    band = jnp.where(keep[None, :, :], band, jnp.zeros((), jnp.bfloat16))
    medium = jnp.einsum(
        "gip,pgc->igc",
        band,
        z_ext.reshape(span_cols, groups_dev, per_group),
        preferred_element_type=jnp.float32,
    ).reshape(rows, width)
    hidden = (query * (medium + skip_gain[None, :] * z_vals.astype(jnp.float32))).astype(
        jnp.bfloat16
    )
    partial_value = jnp.dot(
        hidden,
        lax.all_gather(out_weight, "ctx", axis=1, tiled=True),
        preferred_element_type=jnp.float32,
    )
    return lax.psum_scatter(
        partial_value.astype(jnp.bfloat16), "mp", scatter_dimension=1, tiled=True
    )


def solution(mesh):
    return jax.shard_map(
        on_device,
        mesh=mesh,
        in_specs=(
            P("ctx", None, "mp"),
            P(None, None, "mp"),
            P(None, "mp"),
            P("mp"),
            P("mp", "ctx"),
            P(),
            P(),
        ),
        out_specs=P("ctx", "mp"),
        check_vma=False,
    )
```

profile of v0, /device:TPU:8, one launch (start us, length us, event | category | flops | bytes accessed | tf_op | source)
XLA Modules:
  0.0 223.9 jit_solution(3496047976561221424)
XLA Ops:
  6.5 0.0 copy-start
  6.5 0.0 all-gather.2.cloned.1.call-start
  6.5 0.7 all-gather.2.cloned.1.call-update
  7.3 0.7 compare_reduce_fusion
  8.0 0.1 copy.20
  8.1 0.1 reduce-window.14
  8.1 0.1 fusion.109
  8.3 0.0 copy-done
  8.3 0.6 gather_fusion
  8.9 0.0 copy-start.1
  8.9 0.0 copy-start.5
  9.0 0.0 copy-start.2
  9.0 1.5 select_select_fusion
  10.5 10.3 %all-to-all-start = ((bf16[32,16,3,512]{3,1,2,0:T(8,128)(2,1)}), bf16[32,16,3,512]{3,1,2,0:T(8,128)(2,1)S(1)}, u32[]{:S(2)}, u32[]{:S(2)}) async-start(bf16[32,16,3,512]{3,1,2,0:T(8,128)(2,1)} %select_select_fusion), calls=%async_computation | async-start | bytes 3145728 | tf_op jit(solution)/shard_map/all_to_all | solution.py:53
  20.8 0.0 reduce-scatter.2.cloned.1.call-start
  20.9 0.0 copy-done.1
  20.9 0.2 dynamic-slice_reduce_fusion
  21.1 0.1 broadcast_in_dim.54
  21.1 0.1 broadcast_in_dim.55
  21.2 0.0 copy-done.5
  21.2 0.2 reduce-window.15
  21.5 0.1 select_reduce_fusion
  21.6 0.0 copy-done.2
  21.6 0.6 fusion.111
  22.2 42.6 %all-to-all-done = bf16[32,16,3,512]{3,1,2,0:T(8,128)(2,1)S(1)} async-done(((bf16[32,16,3,512]{3,1,2,0:T(8,128)(2,1)}), bf16[32,16,3,512]{3,1,2,0:T(8,128)(2,1)S(1)}, u32[]{:S(2)}, u32[]{:S(2)}) %all-to-all-start) | async-done | bytes 1572896 | tf_op jit(solution)/shard_map/all_to_all | solution.py:53
  64.8 1.5 gather_fusion.1
  66.4 1.2 copy.22
  67.6 0.2 bitcast_select_fusion
  67.8 3.3 %collective-permute-start = (bf16[6,3,512]{2,0,1:T(8,128)(2,1)S(1)}, bf16[6,3,512]{2,0,1:T(8,128)(2,1)S(1)}, u32[]{:S(2)}, u32[]{:S(2)}) collective-permute-start(bf16[6,3,512]{2,0,1:T(8,128)(2,1)S(1)} %slice.268), channel_id=1, source_target_pairs={{0,16},{16,32},{32,48},{48,64},{64,80},{80,96},{96,112},{112,128},... | collective-permute-start | bytes 55304 | tf_op jit(solution)/shard_map/ppermute | solution.py:10
  71.0 0.0 copy-done.3
  71.0 0.1 rev.3
  71.1 0.6 tile.4
  71.7 0.8 copy.25
  72.5 3.0 %slice.325 = bf16[32,98048]{1,0:T(8,128)(2,1)} slice(bf16[32,98688]{1,0:T(8,128)(2,1)S(1)} %bitcast.156), slice={[0:32], [0:98048]} | slice | bytes 12550144 | tf_op jit(solution)/shard_map/slice | solution.py:75
  75.5 18.4 %reshape.310 = bf16[32,256,383]{2,1,0:T(8,128)(2,1)} reshape(bf16[32,98048]{1,0:T(8,128)(2,1)} %slice.325) | data formatting | bytes 12550144 | tf_op jit(solution)/shard_map/reshape | solution.py:75
  93.9 0.0 collective-permute-done
  93.9 1.6 fusion.7
  95.5 3.8 %collective-permute-start.1 = (bf16[127,512]{1,0:T(8,128)(2,1)S(1)}, bf16[127,512]{1,0:T(8,128)(2,1)S(1)}, u32[]{:S(2)}, u32[]{:S(2)}) collective-permute-start(bf16[127,512]{1,0:T(8,128)(2,1)S(1)} %slice.324), channel_id=1, source_target_pairs={{0,16},{16,32},{32,48},{48,64},{64,80},{80,96},{96,112},{112,128},... | collective-permute-start | bytes 390152 | tf_op jit(solution)/shard_map/ppermute | solution.py:10
  99.3 0.1 broadcast_compare_fusion
  99.5 7.9 %collective-permute-done.1 = bf16[127,512]{1,0:T(8,128)(2,1)S(1)} collective-permute-done((bf16[127,512]{1,0:T(8,128)(2,1)S(1)}, bf16[127,512]{1,0:T(8,128)(2,1)S(1)}, u32[]{:S(2)}, u32[]{:S(2)}) %collective-permute-start.1) | collective-permute-done | bytes 130080 | tf_op jit(solution)/shard_map/ppermute | solution.py:10
  107.3 0.1 pad_maximum_fusion
  107.4 0.2 copy.23
  107.6 5.5 %fusion = f32[32,16,256]{2,1,0:T(8,128)} fusion(bf16[383,32,16]{0,2,1:T(8,128)(2,1)S(1)} %bitcast.158, bf16[32,256,383]{2,1,0:T(8,128)(2,1)} %reshape.310, pred[256,383]{1,0:T(8,128)(4,1)S(1)} %broadcast_compare_fusion), kind=kOutput, calls=%fused_computation.3 | convolution fusion | flops 103538688 | bytes 7289600 | tf_op jit(solution)/shard_map/gip,pgc->igc/dot_general | solution.py:80
  113.1 1.2 copy.24
  114.4 26.8 %all-gather.2.cloned.1.call-done = bf16[512,8192]{1,0:T(8,128)(2,1)} async-done(((bf16[512,256]{1,0:T(8,128)(2,1)}), bf16[512,8192]{1,0:T(8,128)(2,1)}) %all-gather.2.cloned.1.call-update) | async-done | bytes 8388624 | tf_op jit(solution)/shard_map/all_gather | solution.py:91
  141.1 8.1 %convolution_convert_fusion = bf16[256,8192]{1,0:T(8,128)(2,1)} fusion(bf16[512,8192]{1,0:T(8,128)(2,1)} %all-gather.2.cloned.1.call-done, f32[256,512]{1,0:T(8,128)S(1)} %copy.24, bf16[256,512]{1,0:T(8,128)(2,1)S(1)} %fusion.7, bf16[6,3,512]{2,0,1:T(8,128)(2,1)S(1)} %collective-permute-done, bf16[256,3,512]{2,0,1:T(8,128)(2,1)S(1)} %bitcast_select_fusion, ...), kind=kOutput, calls=%fused_computation.2 | convolution fusion | flops 2156920832 | bytes 14466048 | tf_op jit(solution)/shard_map/dot_general | solution.py:89
  149.2 0.0 reduce-scatter.2.cloned.1.call-update
  149.2 67.8 %reduce-scatter.2.cloned.1.call-done = bf16[256,512]{1,0:T(8,128)(2,1)} async-done(((bf16[256,8192]{1,0:T(8,128)(2,1)}), bf16[256,512]{1,0:T(8,128)(2,1)}) %reduce-scatter.2.cloned.1.call-update) | async-done | bytes 262160 | tf_op jit(solution)/shard_map/reduce_scatter | solution.py:94
  (19 shorter events, 0.2 us)
Async XLA Ops:
  6.5 1.7 copy-start
  6.5 134.6 %all-gather.2.cloned.1.call-start = ((), (), s32[]{:S(2)}) async-start(), calls=%async_computation.2 | async-start | bytes 8650752 | tf_op jit(solution)/shard_map/all_gather | solution.py:91
  8.9 11.9 %copy-start.1 = (s32[32,16]{0,1:T(8,128)S(1)}, s32[32,16]{0,1:T(8,128)}, u32[]{:S(2)}) copy-start(s32[32,16]{0,1:T(8,128)} %param.13) | copy-start | bytes 6148
  8.9 12.3 %copy-start.5 = (s32[8]{0:T(128)S(1)}, s32[8]{0:T(128)}, u32[]{:S(2)}) copy-start(s32[8]{0:T(128)} %param.12) | copy-start | bytes 100
  9.0 12.6 %copy-start.2 = (bf16[3,7,512]{2,1,0:T(8,128)(2,1)S(1)}, bf16[3,7,512]{2,1,0:T(8,128)(2,1)}, u32[]{:S(2)}) copy-start(bf16[3,7,512]{2,1,0:T(8,128)(2,1)} %param.8) | copy-start | bytes 64516
  10.5 60.5 %copy-start.3 = (bf16[128,32]{0,1:T(8,128)(2,1)S(1)}, bf16[128,32]{0,1:T(8,128)(2,1)}, u32[]{:S(2)}) copy-start(bf16[128,32]{0,1:T(8,128)(2,1)} %param.9) | copy-start | bytes 24580
  10.5 54.3 %all-to-all-start = ((bf16[32,16,3,512]{3,1,2,0:T(8,128)(2,1)}), bf16[32,16,3,512]{3,1,2,0:T(8,128)(2,1)S(1)}, u32[]{:S(2)}, u32[]{:S(2)}) async-start(bf16[32,16,3,512]{3,1,2,0:T(8,128)(2,1)} %select_select_fusion), calls=%async_computation | async-start | bytes 3145728 | tf_op jit(solution)/shard_map/all_to_all | solution.py:53
  20.8 196.2 %reduce-scatter.2.cloned.1.call-start = ((), (), s32[]{:S(2)}) async-start(), calls=%async_computation.3 | async-start | bytes 4456448 | tf_op jit(solution)/shard_map/reduce_scatter | solution.py:94
  21.6 72.3 %copy-start.4 = (f32[256]{0:T(256)}, f32[256]{0:T(256)S(1)}, u32[]{:S(2)}) copy-start(f32[256]{0:T(256)S(1)} %get-tuple-element.38) | copy-start | bytes 3076
  67.8 26.1 %collective-permute-start = (bf16[6,3,512]{2,0,1:T(8,128)(2,1)S(1)}, bf16[6,3,512]{2,0,1:T(8,128)(2,1)S(1)}, u32[]{:S(2)}, u32[]{:S(2)}) collective-permute-start(bf16[6,3,512]{2,0,1:T(8,128)(2,1)S(1)} %slice.268), channel_id=1, source_target_pairs={{0,16},{16,32},{32,48},{48,64},{64,80},{80,96},{96,112},{112,128},... | collective-permute-start | bytes 55304 | tf_op jit(solution)/shard_map/ppermute | solution.py:10
  95.5 11.8 %collective-permute-start.1 = (bf16[127,512]{1,0:T(8,128)(2,1)S(1)}, bf16[127,512]{1,0:T(8,128)(2,1)S(1)}, u32[]{:S(2)}, u32[]{:S(2)}) collective-permute-start(bf16[127,512]{1,0:T(8,128)(2,1)S(1)} %slice.324), channel_id=1, source_target_pairs={{0,16},{16,32},{32,48},{48,64},{64,80},{80,96},{96,112},{112,128},... | collective-permute-start | bytes 390152 | tf_op jit(solution)/shard_map/ppermute | solution.py:10
Sparse Core Ops, SparseCore 0:
  10.4 130.6 all-gather.1
  149.4 67.6 reduce-scatter.1
where the time goes:
time: 224 us
  waiting for transfers between devices  146 us (65%)
  local copies, waits for them, and re-layouts  28.8 us (13%)
  starting transfers between devices  17.4 us (8%)
  matrix products  13.6 us (6%)
  between operations  13.6 us (6%)
  other arithmetic  4.66 us (2%)
    reduce_scatter x1, waiting for transfers between devices, on_device(): lax.psum_scatter(partial_value.astype(jnp.bfloat16), 'mp', scatter_dimens...  67.8 us
    all_to_all x1, waiting for transfers between devices, on_device(): lax.all_to_all(outgoing, 'ctx', split_axis=0, concat_axis=0, tiled=True)  42.6 us
    all_gather x1, waiting for transfers between devices, on_device(): lax.all_gather(out_weight, 'ctx', axis=1, tiled=True)  26.8 us
    reshape x1, local copies, waits for them, and re-layouts, on_device(): jnp.tile(line, (1, rows + 1))[:, :rows * span_cols]  18.4 us
    all_to_all x1, starting transfers between devices, on_device(): lax.all_to_all(outgoing, 'ctx', split_axis=0, concat_axis=0, tiled=True)  10.3 us
    dot_general x1, matrix products, on_device(): jnp.dot(hidden, lax.all_gather(out_weight, 'ctx', axis=1, tiled=True), pr...  8.11 us
    ppermute x2, waiting for transfers between devices, passed_along(): return lax.ppermute(block, axis, route)  7.88 us
    ppermute x2, starting transfers between devices, passed_along(): return lax.ppermute(block, axis, route)  7.08 us
  transfers between devices with their start and end apart: 5, of which 4 were waited for; matrix products, arithmetic and copies ran while one was open for 17% of the time, Pallas kernels for 0%

commit v1 on v0

--- a/solution.py
+++ b/solution.py
@@ -88,7 +88,9 @@
     )
     partial_value = jnp.dot(
         hidden,
-        lax.all_gather(out_weight, "ctx", axis=1, tiled=True),
+        jnp.concatenate(
+            lax.all_to_all(jnp.stack([out_weight] * lax.axis_size("ctx")), "ctx", 0, 0), axis=1
+        ),
         preferred_element_type=jnp.float32,
     )
     return lax.psum_scatter(

time: 224 us -> 359 us (1.60)
  the two profiles are of different devices: /device:TPU:8 before, /device:TPU:6 now
where the time goes in v1:
time: 359 us; the launch traced here: 358 us
  waiting for transfers between devices  265 us (74%)
  local copies, waits for them, and re-layouts  33.5 us (9%)
  starting transfers between devices  26 us (7%)
  matrix products  14.4 us (4%)
  between operations  13.6 us (4%)
  other arithmetic  5.35 us (1%)
    ppermute x2, waiting for transfers between devices, passed_along(): return lax.ppermute(block, axis, route)  155 us
    reduce_scatter x1, waiting for transfers between devices, on_device(): lax.psum_scatter(partial_value.astype(jnp.bfloat16), 'mp', scatter_dimens...  72.4 us
    all_to_all x1, waiting for transfers between devices, on_device(): lax.all_to_all(outgoing, 'ctx', split_axis=0, concat_axis=0, tiled=True)  38.2 us
    reshape x1, local copies, waits for them, and re-layouts, on_device(): jnp.tile(line, (1, rows + 1))[:, :rows * span_cols]  18.4 us
    all_to_all x1, starting transfers between devices, on_device(): lax.all_to_all(outgoing, 'ctx', split_axis=0, concat_axis=0, tiled=True)  10.2 us
    ppermute x2, starting transfers between devices, passed_along(): return lax.ppermute(block, axis, route)  10.1 us
    dot_general x1, matrix products, on_device(): jnp.dot(hidden, jnp.concatenate(lax.all_to_all(jnp.stack([out_weight] * l...  9.77 us
  transfers between devices with their start and end apart: 5, of which 4 were waited for; matrix products, arithmetic and copies ran while one was open for 10% of the time, Pallas kernels for 0%

profile of v1, /device:TPU:6, one launch (start us, length us, event | category | flops | bytes accessed | tf_op | source)
XLA Modules:
  0.0 358.1 jit_solution(443335233735151962)
XLA Ops:
  6.5 0.0 copy-start
  6.5 0.8 compare_reduce_fusion
  7.4 0.1 copy.22
  7.5 0.1 reduce-window.14
  7.5 0.1 fusion.139
  7.7 0.3 copy-done
  8.0 0.6 gather_fusion
  8.6 1.4 select_select_fusion
  10.0 10.2 %all-to-all-start = ((bf16[32,16,3,512]{3,1,2,0:T(8,128)(2,1)}), bf16[32,16,3,512]{3,1,2,0:T(8,128)(2,1)S(1)}, u32[]{:S(2)}, u32[]{:S(2)}) async-start(bf16[32,16,3,512]{3,1,2,0:T(8,128)(2,1)} %select_select_fusion), calls=%async_computation | async-start | bytes 3145728 | tf_op jit(solution)/shard_map/all_to_all | solution.py:53
  20.2 1.1 copy.27
  21.3 38.2 %all-to-all-done = bf16[32,16,3,512]{3,1,2,0:T(8,128)(2,1)S(1)} async-done(((bf16[32,16,3,512]{3,1,2,0:T(8,128)(2,1)}), bf16[32,16,3,512]{3,1,2,0:T(8,128)(2,1)S(1)}, u32[]{:S(2)}, u32[]{:S(2)}) %all-to-all-start) | async-done | bytes 1572896 | tf_op jit(solution)/shard_map/all_to_all | solution.py:53
  59.5 4.2 %stack.2 = bf16[32,512,256]{1,2,0:T(8,128)(2,1)} broadcast(bf16[512,256]{0,1:T(8,128)(2,1)S(1)} %copy.27), dimensions={1,2} | broadcast | bytes 8650752 | tf_op jit(solution)/shard_map/stack | solution.py:92
  63.7 0.0 copy-start.5
  63.7 5.8 %all-to-all-start.1 = ((bf16[32,512,256]{1,2,0:T(8,128)(2,1)}), bf16[32,512,256]{1,2,0:T(8,128)(2,1)}, u32[]{:S(2)}, u32[]{:S(2)}) async-start(bf16[32,512,256]{1,2,0:T(8,128)(2,1)} %stack.2), calls=%async_computation.1 | async-start | bytes 16777216 | tf_op jit(solution)/shard_map/all_to_all | solution.py:92
  69.5 0.0 copy-start.3
  69.5 0.0 reduce-scatter.2.cloned.1.call-start
  69.5 0.0 copy-done.5
  69.5 0.2 reduce-window.15
  69.7 0.0 copy-done.1
  69.7 0.2 dynamic-slice_reduce_fusion
  69.9 0.1 broadcast_in_dim.54
  70.0 0.1 broadcast_in_dim.55
  70.1 0.1 select_reduce_fusion
  70.2 0.0 copy-done.2
  70.3 1.5 gather_fusion.1
  71.8 1.2 copy.24
  73.0 0.2 bitcast_select_fusion
  73.2 3.4 collective-permute-start
  76.6 0.0 copy-done.3
  76.6 0.1 rev.3
  76.7 0.6 tile.4
  77.3 0.8 copy.28
  78.1 3.0 slice.346
  81.1 18.4 %reshape.563 = bf16[32,256,383]{2,1,0:T(8,128)(2,1)} reshape(bf16[32,98048]{1,0:T(8,128)(2,1)} %slice.346) | data formatting | bytes 12550144 | tf_op jit(solution)/shard_map/reshape | solution.py:75
  99.5 152.4 %collective-permute-done = bf16[6,3,512]{2,0,1:T(8,128)(2,1)S(1)} collective-permute-done((bf16[6,3,512]{2,0,1:T(8,128)(2,1)S(1)}, bf16[6,3,512]{2,0,1:T(8,128)(2,1)S(1)}, u32[]{:S(2)}, u32[]{:S(2)}) %collective-permute-start) | collective-permute-done | bytes 18464 | tf_op jit(solution)/shard_map/ppermute | solution.py:10
  251.9 2.2 fusion.13
  254.2 6.7 %collective-permute-start.1 = (bf16[127,512]{1,0:T(8,128)(2,1)S(1)}, bf16[127,512]{1,0:T(8,128)(2,1)S(1)}, u32[]{:S(2)}, u32[]{:S(2)}) collective-permute-start(bf16[127,512]{1,0:T(8,128)(2,1)S(1)} %slice.345), channel_id=1, source_target_pairs={{0,16},{16,32},{32,48},{48,64},{64,80},{80,96},{96,112},{112,128},... | collective-permute-start | bytes 390152 | tf_op jit(solution)/shard_map/ppermute | solution.py:10
  260.8 0.1 broadcast_compare_fusion
  261.0 2.2 collective-permute-done.1
  263.2 0.1 pad_maximum_fusion
  263.2 0.9 copy.25
  264.2 4.7 %fusion = f32[32,16,256]{2,1,0:T(8,128)S(1)} fusion(bf16[383,32,16]{0,2,1:T(8,128)(2,1)} %bitcast.190, bf16[32,256,383]{2,1,0:T(8,128)(2,1)} %reshape.563, pred[256,383]{1,0:T(8,128)(4,1)S(1)} %broadcast_compare_fusion), kind=kOutput, calls=%fused_computation.3 | convolution fusion | flops 103538688 | bytes 7289600 | tf_op jit(solution)/shard_map/gip,pgc->igc/dot_general | solution.py:80
  268.8 0.2 copy.26
  269.1 0.0 all-to-all-done.1
  269.1 0.0 copy-done.4
  269.1 9.8 %convolution_convert_fusion = bf16[256,8192]{1,0:T(8,128)(2,1)} fusion(bf16[512,8192]{0,1:T(8,128)(2,1)} %bitcast.47, f32[256,1,512]{2,0,1:T(8,128)S(1)} %copy.26, bf16[6,3,512]{2,0,1:T(8,128)(2,1)S(1)} %collective-permute-done, bf16[256,3,512]{2,0,1:T(8,128)(2,1)S(1)} %bitcast_select_fusion, bf16[256,1,512]{2,0,1:T(8,128)(2,1)} %get-tuple-element.8, ...), kind=kOutput, calls=%fused_computation.2 | convolution fusion | flops 2167799808 | bytes 15019008 | tf_op jit(solution)/shard_map/dot_general | solution.py:89
  278.9 0.0 reduce-scatter.2.cloned.1.call-update
  278.9 72.4 %reduce-scatter.2.cloned.1.call-done = bf16[256,512]{1,0:T(8,128)(2,1)} async-done(((bf16[256,8192]{1,0:T(8,128)(2,1)}), bf16[256,512]{1,0:T(8,128)(2,1)}) %reduce-scatter.2.cloned.1.call-update) | async-done | bytes 262160 | tf_op jit(solution)/shard_map/reduce_scatter | solution.py:96
  (20 shorter events, 0.2 us)
Async XLA Ops:
  6.5 1.4 copy-start
  10.0 49.5 %all-to-all-start = ((bf16[32,16,3,512]{3,1,2,0:T(8,128)(2,1)}), bf16[32,16,3,512]{3,1,2,0:T(8,128)(2,1)S(1)}, u32[]{:S(2)}, u32[]{:S(2)}) async-start(bf16[32,16,3,512]{3,1,2,0:T(8,128)(2,1)} %select_select_fusion), calls=%async_computation | async-start | bytes 3145728 | tf_op jit(solution)/shard_map/all_to_all | solution.py:53
  63.7 5.8 %copy-start.5 = (s32[8]{0:T(128)S(1)}, s32[8]{0:T(128)}, u32[]{:S(2)}) copy-start(s32[8]{0:T(128)} %param.12) | copy-start | bytes 100
  63.7 6.0 %copy-start.1 = (s32[32,16]{0,1:T(8,128)S(1)}, s32[32,16]{0,1:T(8,128)}, u32[]{:S(2)}) copy-start(s32[32,16]{0,1:T(8,128)} %param.13) | copy-start | bytes 6148
  63.7 6.5 %copy-start.2 = (bf16[3,7,512]{2,1,0:T(8,128)(2,1)S(1)}, bf16[3,7,512]{2,1,0:T(8,128)(2,1)}, u32[]{:S(2)}) copy-start(bf16[3,7,512]{2,1,0:T(8,128)(2,1)} %param.8) | copy-start | bytes 64516
  63.7 205.4 %all-to-all-start.1 = ((bf16[32,512,256]{1,2,0:T(8,128)(2,1)}), bf16[32,512,256]{1,2,0:T(8,128)(2,1)}, u32[]{:S(2)}, u32[]{:S(2)}) async-start(bf16[32,512,256]{1,2,0:T(8,128)(2,1)} %stack.2), calls=%async_computation.1 | async-start | bytes 16777216 | tf_op jit(solution)/shard_map/all_to_all | solution.py:92
  69.5 7.1 %copy-start.3 = (bf16[128,32]{0,1:T(8,128)(2,1)S(1)}, bf16[128,32]{0,1:T(8,128)(2,1)}, u32[]{:S(2)}) copy-start(bf16[128,32]{0,1:T(8,128)(2,1)} %param.9) | copy-start | bytes 24580
  69.5 281.8 %reduce-scatter.2.cloned.1.call-start = ((), (), s32[]{:S(2)}) async-start(), calls=%async_computation.3 | async-start | bytes 4456448 | tf_op jit(solution)/shard_map/reduce_scatter | solution.py:96
  73.2 178.7 %collective-permute-start = (bf16[6,3,512]{2,0,1:T(8,128)(2,1)S(1)}, bf16[6,3,512]{2,0,1:T(8,128)(2,1)S(1)}, u32[]{:S(2)}, u32[]{:S(2)}) collective-permute-start(bf16[6,3,512]{2,0,1:T(8,128)(2,1)S(1)} %slice.289), channel_id=1, source_target_pairs={{0,16},{16,32},{32,48},{48,64},{64,80},{80,96},{96,112},{112,128},... | collective-permute-start | bytes 55304 | tf_op jit(solution)/shard_map/ppermute | solution.py:10
  254.2 9.0 %collective-permute-start.1 = (bf16[127,512]{1,0:T(8,128)(2,1)S(1)}, bf16[127,512]{1,0:T(8,128)(2,1)S(1)}, u32[]{:S(2)}, u32[]{:S(2)}) collective-permute-start(bf16[127,512]{1,0:T(8,128)(2,1)S(1)} %slice.345), channel_id=1, source_target_pairs={{0,16},{16,32},{32,48},{48,64},{64,80},{80,96},{96,112},{112,128},... | collective-permute-start | bytes 390152 | tf_op jit(solution)/shard_map/ppermute | solution.py:10
  264.2 4.9 %copy-start.4 = (f32[512]{0:T(512)S(1)}, f32[512]{0:T(512)}, u32[]{:S(2)}) copy-start(f32[512]{0:T(512)} %param.10) | copy-start | bytes 6148
Sparse Core Ops, SparseCore 0:
  279.0 72.2 reduce-scatter.1
